TPU v7x, 256 devices: a whole 4x4x8 slice. The times are simulated.
256 devices in a mesh: dp: 8 (over z), expert: 32 (over x, y, core).
Axes of the slice: x: 4, y: 4, z: 8, core: 2. Of those that a mesh axis runs over, the one named last changes fastest.
Arguments:
- tokens: bfloat16 [256, 212, 1024], P(('dp', 'expert')), may hold values from -6 to 6
- expert_ids: int32 [256, 212, 1], P(('dp', 'expert')), may hold values from 0 to 31; in each aligned block of 212 rows (0 to 211, 212 to 423, ..., all dimensions but the last counted through in order) at most 9 rows name the same one
- caption_lengths: int32 [256], P(('dp', 'expert')), may hold values from 1 to 16, as said below
- layer_norm_gain: float32 [1024], replicated, may hold values from 0.5 to 1.5
- router: float32 [1024, 32], replicated, may hold values from -0.1875 to 0.1875
- w_up: bfloat16 [32, 1024, 4096], P('expert', None, 'dp'), may hold values from -0.1875 to 0.1875
- w_down: bfloat16 [32, 4096, 1024], P('expert', 'dp'), may hold values from -0.09375 to 0.09375
- logit_scale: float32 [1], replicated, may hold values from 5 to 20
- logit_bias: float32 [1], replicated, may hold values from -4 to -1.5
Outputs:
- loss: float32 [1], replicated
- grad_tokens: bfloat16 [256, 212, 1024], P(('dp', 'expert'))
- grad_up: float32 [32, 1024, 4096], P('expert', None, 'dp')
- grad_down: float32 [32, 4096, 1024], P('expert', 'dp')
- grad_router: float32 [1024, 32], replicated
- layer_gain_gradient: float32 [1024], replicated
Inputs may be any that keep to these rules, and one draw needn't show every extreme that they name: `expert_ids`: among the rows of one device (aligned blocks of 212 rows, devices ordered by dp then expert) no expert is named more than 9 times, a bound that some block reaches. `caption_lengths`: some caption has all 16 tokens.
All inputs are finite; a program needn't handle non-finite values.
Results may differ from a plain program's by a relative error of at most 0.009.
Values may be sent and summed in bfloat16 or wider, within the bound.
No kernel may reach another device: no remote copies, remote signals or barrier semaphores. Data moves between devices by JAX's collectives and lax.ppermute only.
A program may use at most 128 MiB of HBM per device.

v0:
```python
import jax
import jax.numpy as jnp
from jax import lax
from jax.sharding import PartitionSpec as P

D = 1024
PATCH = 196
CAPLEN = 16
SEQ = 212
eps = 1e-06
loss_scale = 1024.0


def gelu_slope(pre):
    return (
        0.5 * (1.0 + lax.erf(pre * 0.7071067811865476))
        + pre * jnp.exp(-0.5 * pre * pre) * 0.3989422804014327
    )


def deliver(buffer, experts, slots):
    width = buffer.shape[-1]
    sent = lax.all_to_all(
        buffer.reshape(experts, 1, slots, width), "expert", split_axis=0, concat_axis=1, tiled=True
    )
    shaped = sent.reshape(sent.shape[0], 1, sent.shape[1], slots, width)
    whole = lax.all_gather(shaped, "dp", axis=1, tiled=True)
    return whole.reshape(whole.shape[0], -1, width)


def give_back(partial_value, n_dp, n_expert, slots):
    local = partial_value.shape[0]
    width = partial_value.shape[-1]
    summed = lax.psum_scatter(
        partial_value.reshape(local, n_dp, n_expert * slots, width).astype(jnp.bfloat16),
        "dp",
        scatter_dimension=1,
        tiled=True,
    )
    rounded = summed.reshape(local, n_expert, slots, width)
    returned = lax.all_to_all(rounded, "expert", split_axis=1, concat_axis=0, tiled=True)
    return returned.reshape(-1, width)


def body(
    tokens,
    expert_ids,
    caption_lengths,
    layer_norm_gain,
    router,
    w_up,
    w_down,
    logit_scale,
    logit_bias,
):
    n_dp = lax.axis_size("dp")
    n_expert = lax.axis_size("expert")
    pair_dev = tokens.shape[0]
    rows = pair_dev * SEQ
    experts = router.shape[1]
    slots = rows * 4 // (3 * experts) + 1
    pairs_all = pair_dev * n_dp * n_expert
    input_rows = tokens.reshape(rows, D).astype(jnp.float32)
    input_mean = jnp.mean(input_rows, axis=1, keepdims=True)
    var_x = jnp.mean((input_rows - input_mean) ** 2, axis=1, keepdims=True)
    inverse_deviation = 1.0 / jnp.sqrt(var_x + eps)
    centered_scaled_input = (input_rows - input_mean) * inverse_deviation
    normalized_input = (centered_scaled_input * layer_norm_gain).astype(jnp.bfloat16)
    ids = expert_ids.reshape(rows)
    onehot = (ids[:, None] == jnp.arange(experts, dtype=jnp.int32)[None, :]).astype(jnp.int32)
    slot = jnp.sum((jnp.cumsum(onehot, axis=0) - 1) * onehot, axis=1)
    dest = ids * slots + slot
    onehot_f = onehot.astype(jnp.float32)
    buffer = jnp.zeros((experts * slots, D), jnp.bfloat16).at[dest].set(normalized_input)
    gathered = deliver(buffer, experts, slots)
    pre = jnp.einsum("erd,edf->erf", gathered, w_up, preferred_element_type=jnp.float32)
    act = jax.nn.gelu(pre, approximate=False).astype(jnp.bfloat16)
    partial_value = jnp.einsum("erf,efd->erd", act, w_down, preferred_element_type=jnp.float32)
    moe = give_back(partial_value, n_dp, n_expert, slots)[dest].astype(jnp.float32)
    xnf = normalized_input.astype(jnp.float32)
    router_logits = jnp.dot(xnf, router, precision=lax.Precision.HIGHEST)
    gate = jax.nn.sigmoid(jnp.sum(router_logits * onehot_f, axis=1))
    y = (input_rows + gate[:, None] * moe).reshape(pair_dev, SEQ, D)
    img = jnp.mean(y[:, :PATCH], axis=1)
    lengths = caption_lengths.astype(jnp.float32)
    mask = (jnp.arange(CAPLEN, dtype=jnp.int32)[None, :] < caption_lengths[:, None]).astype(
        jnp.float32
    )
    txt = jnp.sum(y[:, PATCH:] * mask[:, :, None], axis=1) / lengths[:, None]
    ru = jnp.sqrt(jnp.mean(img * img, axis=1, keepdims=True) + eps)
    rv = jnp.sqrt(jnp.mean(txt * txt, axis=1, keepdims=True) + eps)
    u = img / ru
    v = txt / rv
    scale = logit_scale[0]
    first = lax.axis_index(("dp", "expert")) * pair_dev
    mine = first + jnp.arange(pair_dev, dtype=jnp.int32)
    every = jnp.arange(pairs_all, dtype=jnp.int32)
    own_sign = jnp.where(mine[:, None] == every[None, :], 1.0, -1.0)
    v_all = lax.all_gather(v, ("dp", "expert"), axis=0, tiled=True)
    logits = scale * jnp.dot(u, v_all.T, precision=lax.Precision.HIGHEST) / D + logit_bias[0]
    loss_term = -jnp.sum(jax.nn.log_sigmoid(own_sign * logits)) / pairs_all
    coef = -(loss_scale / pairs_all) * own_sign * jax.nn.sigmoid(-own_sign * logits)
    du = scale / D * jnp.dot(coef, v_all, precision=lax.Precision.HIGHEST)
    dv_terms = scale / D * jnp.dot(coef.T, u, precision=lax.Precision.HIGHEST)
    dv = lax.psum_scatter(dv_terms, ("dp", "expert"), scatter_dimension=0, tiled=True)
    dimg = (du - u * jnp.mean(du * u, axis=1, keepdims=True)) / ru
    dtxt = (dv - v * jnp.mean(dv * v, axis=1, keepdims=True)) / rv
    dy_img = jnp.broadcast_to(dimg[:, None, :] / PATCH, (pair_dev, PATCH, D))
    dy_txt = (dtxt / lengths[:, None])[:, None, :] * mask[:, :, None]
    dy = jnp.concatenate([dy_img, dy_txt], axis=1).reshape(rows, D)
    dmoe = (gate[:, None] * dy).astype(jnp.bfloat16)
    dgl = jnp.sum(dy * moe, axis=1) * gate * (1.0 - gate)
    router_part = jnp.dot(xnf.T, onehot_f * dgl[:, None], precision=lax.Precision.HIGHEST)
    grad_buffer = jnp.zeros((experts * slots, D), jnp.bfloat16).at[dest].set(dmoe)
    gathered_grads = deliver(grad_buffer, experts, slots)
    dact = jnp.einsum("erd,efd->erf", gathered_grads, w_down, preferred_element_type=jnp.float32)
    dpre = (dact * gelu_slope(pre)).astype(jnp.bfloat16)
    grad_down = jnp.einsum("erf,erd->efd", act, gathered_grads, preferred_element_type=jnp.float32)
    grad_up = jnp.einsum("erd,erf->edf", gathered, dpre, preferred_element_type=jnp.float32)
    back_partial = jnp.einsum("erf,edf->erd", dpre, w_up, preferred_element_type=jnp.float32)
    dxe = give_back(back_partial, n_dp, n_expert, slots)[dest].astype(jnp.float32)
    router_rows = jnp.dot(onehot_f, router.T, precision=lax.Precision.HIGHEST)
    gradient_normalized_input = dxe + dgl[:, None] * router_rows
    gain_partial_term = jnp.sum(gradient_normalized_input * centered_scaled_input, axis=0)
    scaled_output_gradient = gradient_normalized_input * layer_norm_gain
    normed_input_gradient = (
        scaled_output_gradient
        - jnp.mean(scaled_output_gradient, axis=1, keepdims=True)
        - centered_scaled_input
        * jnp.mean(scaled_output_gradient * centered_scaled_input, axis=1, keepdims=True)
    ) * inverse_deviation
    grad_tokens = (dy + normed_input_gradient).astype(jnp.bfloat16).reshape(pair_dev, SEQ, D)
    loss, grad_router, layer_gain_gradient = lax.psum(
        (loss_term, router_part, gain_partial_term), ("dp", "expert")
    )
    return (loss.reshape(1), grad_tokens, grad_up, grad_down, grad_router, layer_gain_gradient)


def solution(mesh):
    return jax.shard_map(
        body,
        mesh=mesh,
        in_specs=(
            P(("dp", "expert"), None, None),
            P(("dp", "expert"), None, None),
            P(("dp", "expert")),
            P(),
            P(),
            P("expert", None, "dp"),
            P("expert", "dp", None),
            P(),
            P(),
        ),
        out_specs=(
            P(),
            P(("dp", "expert"), None, None),
            P("expert", None, "dp"),
            P("expert", "dp", None),
            P(),
            P(),
        ),
        check_vma=False,
    )
```

profile of v0, /device:TPU:8, one launch (start us, length us, event | category | flops | bytes accessed | tf_op | source)
XLA Modules:
  0.0 1022.8 jit_solution(2046483523152713916)
XLA Ops:
  12.8 2.3 scatter_custom_fusion
  15.4 22.9 %all_to_all.16 = bf16[32,1,9,1024]{3,2,1,0:T(8,128)(2,1)S(1)} all-to-all(bf16[32,1,9,1024]{3,2,1,0:T(8,128)(2,1)S(1)} %bitcast.149), channel_id=1, replica_groups=mesh['dp'=8,'expert'=32] {'expert'}, dimensions={0} | all-to-all | bytes 1179648 | tf_op jit(solution)/shard_map/all_to_all | solution.py:23
  39.7 60.3 %all-gather.7.cloned.1.call-done = bf16[256,1,9,1024]{3,0,2,1:T(8,128)(2,1)} async-done(((bf16[32,1,9,1024]{3,0,2,1:T(8,128)(2,1)}), bf16[256,1,9,1024]{3,0,2,1:T(8,128)(2,1)}) %all-gather.7.cloned.1.call-update) | async-done | bytes 4718608 | tf_op jit(solution)/shard_map/all_gather | solution.py:27
  100.0 8.7 copy.22
  108.7 9.8 reshape.491
  118.6 14.9 %fusion.2 = (bf16[2304,512]{1,0:T(8,128)(2,1)S(1)}, f32[2304,512]{1,0:T(8,128)}) fusion(bf16[2304,1024]{1,0:T(8,128)(2,1)} %reshape.491, bf16[1,1024,512]{2,1,0:T(8,128)(2,1)S(1)} %copy-done), kind=kOutput, calls=%fused_computation.9 | convolution fusion | flops 2492596224 | bytes 12845056 | tf_op jit(solution)/shard_map/erd,edf->erf/dot_general | solution.py:76
  134.8 4.2 convert_bitcast_fusion.1
  139.8 58.3 %reduce-scatter.3.cloned.1.call-done = bf16[1,1,288,1024]{3,2,1,0:T(8,128)(2,1)} async-done(((bf16[1,8,288,1024]{3,2,1,0:T(8,128)(2,1)}), bf16[1,1,288,1024]{3,2,1,0:T(8,128)(2,1)}) %reduce-scatter.3.cloned.1.call-update) | async-done | bytes 589840 | tf_op jit(solution)/shard_map/reduce_scatter | solution.py:34
  198.1 2.2 reshape.494
  200.2 7.4 all-to-all-start.1
  208.8 14.4 %all-to-all-done.1 = bf16[1,32,9,1024]{3,2,0,1:T(8,128)(2,1)S(1)} async-done(((bf16[1,32,9,1024]{3,2,0,1:T(8,128)(2,1)}), bf16[1,32,9,1024]{3,2,0,1:T(8,128)(2,1)S(1)}, u32[]{:S(2)}, u32[]{:S(2)}) %all-to-all-start.1) | async-done | bytes 589856 | tf_op jit(solution)/shard_map/all_to_all | solution.py:41
  229.8 95.7 %all-gather.9.cloned.1.call-done = f32[262144]{0:T(1024)} async-done(((f32[1024]{0:T(1024)}), f32[262144]{0:T(1024)}) %all-gather.9.cloned.1.call-update) | async-done | bytes 1048592 | tf_op jit(solution)/shard_map/all_gather | solution.py:99
  331.5 254.7 %all-reduce.8.cloned.1.call-done = f32[256,1024]{1,0:T(8,128)} async-done(((f32[256,1024]{1,0:T(8,128)}), f32[256,1024]{1,0:T(8,128)}) %all-reduce.8.cloned.1.call-update) | async-done | bytes 1048592
  589.2 2.5 scatter_custom_fusion.1
  593.0 22.3 %all_to_all.17 = bf16[32,1,9,1024]{3,2,1,0:T(8,128)(2,1)S(1)} all-to-all(bf16[32,1,9,1024]{3,2,1,0:T(8,128)(2,1)S(1)} %bitcast.150), channel_id=1, replica_groups=mesh['dp'=8,'expert'=32] {'expert'}, dimensions={0} | all-to-all | bytes 1179648 | tf_op jit(solution)/shard_map/all_to_all | solution.py:23
  616.6 57.0 %all-gather.11.cloned.1.call-done = bf16[256,1,9,1024]{3,0,2,1:T(8,128)(2,1)} async-done(((bf16[32,1,9,1024]{3,0,2,1:T(8,128)(2,1)}), bf16[256,1,9,1024]{3,0,2,1:T(8,128)(2,1)}) %all-gather.11.cloned.1.call-update) | async-done | bytes 4718608 | tf_op jit(solution)/shard_map/all_gather | solution.py:27
  673.6 8.7 copy.26
  682.3 9.9 reshape.500
  692.2 7.0 fusion.14
  700.6 4.4 convert_bitcast_fusion
  707.3 7.0 convolution_bitcast_fusion
  714.3 49.8 %reduce-scatter.5.cloned.1.call-done = bf16[1,1,288,1024]{3,2,1,0:T(8,128)(2,1)} async-done(((bf16[1,8,288,1024]{3,2,1,0:T(8,128)(2,1)}), bf16[1,1,288,1024]{3,2,1,0:T(8,128)(2,1)}) %reduce-scatter.5.cloned.1.call-update) | async-done | bytes 589840 | tf_op jit(solution)/shard_map/reduce_scatter | solution.py:34
  764.1 2.2 reshape.501
  766.3 7.5 all-to-all-start.3
  773.7 7.1 convolution_bitcast_fusion.1
  780.8 8.6 all-to-all-done.3
  789.4 1.4 reshape.502
  790.8 2.0 gather_fusion.1
  792.8 2.3 fusion.37
  796.3 75.8 %all-reduce.2 = (f32[1]{0:T(128)}, f32[1024]{0:T(1024)}) all-reduce(f32[1]{0:T(128)} %bitcast.20, f32[1024]{0:T(1024)S(1)} %get-tuple-element.6), channel_id=1, replica_groups=mesh['dp'=8,'expert'=32] {'dp','expert'}, use_global_device_ids=true, to_apply=%region_13.14 | all-reduce | flops 1025 | bytes 8200 | tf_op jit(solution)/shard_map/psum | solution.py:133
  872.1 142.3 %all-reduce.6.cloned.1.call-done = f32[1024,32]{0,1:T(8,128)} async-done(((f32[1024,32]{0,1:T(8,128)}), f32[1024,32]{0,1:T(8,128)}) %all-reduce.6.cloned.1.call-update) | async-done | bytes 131088 | tf_op jit(solution)/shard_map/psum | solution.py:133
  1014.4 1.6 copy.37
  (117 shorter events, 27.8 us)
Async XLA Ops:
  7.2 111.4 %copy-start = (bf16[1,1024,512]{2,1,0:T(8,128)(2,1)S(1)}, bf16[1,1024,512]{2,1,0:T(8,128)(2,1)}, u32[]{:S(2)}) copy-start(bf16[1,1024,512]{2,1,0:T(8,128)(2,1)} %param.14) | copy-start | bytes 3145732
  7.2 92.8 %all-gather.7.cloned.1.call-start = ((), (), s32[]{:S(2)}) async-start(), calls=%async_computation.9 | async-start | bytes 5308416 | tf_op jit(solution)/shard_map/all_gather | solution.py:27
  8.5 199.2 %copy-start.11 = (f32[212]{0:T(256)}, f32[212]{0:T(256)S(1)}, u32[]{:S(2)}) copy-start(f32[212]{0:T(256)S(1)} %broadcast_multiply_fusion.3) | copy-start | bytes 2548
  9.8 197.9 %copy-start.15 = (f32[212]{0:T(256)}, f32[212]{0:T(256)S(1)}, u32[]{:S(2)}) copy-start(f32[212]{0:T(256)S(1)} %add_rsqrt_fusion) | copy-start | bytes 2548
  12.8 127.0 %copy-start.22 = (s32[212,1]{0,1:T(1,128)}, s32[212,1]{0,1:T(1,128)S(1)}, u32[]{:S(2)}) copy-start(s32[212,1]{0,1:T(1,128)S(1)} %compare_select_fusion) | copy-start | bytes 2548
  39.4 158.6 %reduce-scatter.3.cloned.1.call-start = ((), (), s32[]{:S(2)}) async-start(), calls=%async_computation.6 | async-start | bytes 5308416 | tf_op jit(solution)/shard_map/reduce_scatter | solution.py:34
  118.6 16.3 %copy-start.25 = (bf16[1,512,1024]{2,1,0:T(8,128)(2,1)S(1)}, bf16[1,512,1024]{2,1,0:T(8,128)(2,1)}, u32[]{:S(2)}) copy-start(bf16[1,512,1024]{2,1,0:T(8,128)(2,1)} %param.15) | copy-start | bytes 3145732
  133.4 1.4 copy-start.27
  139.0 68.7 %copy-start.1 = (bf16[1,212,1024]{2,1,0:T(8,128)(2,1)S(1)}, bf16[1,212,1024]{2,1,0:T(8,128)(2,1)}, u32[]{:S(2)}) copy-start(bf16[1,212,1024]{2,1,0:T(8,128)(2,1)} %param.9) | copy-start | bytes 1302532
  139.0 68.7 %copy-start.9 = (f32[1024]{0:T(1024)S(1)}, f32[1024]{0:T(1024)}, u32[]{:S(2)}) copy-start(f32[1024]{0:T(1024)} %param.12) | copy-start | bytes 12292
  139.0 69.0 %copy-start.7 = (f32[1024,32]{0,1:T(8,128)S(1)}, f32[1024,32]{0,1:T(8,128)}, u32[]{:S(2)}) copy-start(f32[1024,32]{0,1:T(8,128)} %param.13) | copy-start | bytes 393220
  139.0 69.0 %copy-start.13 = (s32[1,212,1]{1,2,0:T(1,128)S(1)}, s32[1,212,1]{1,2,0:T(1,128)}, u32[]{:S(2)}) copy-start(s32[1,212,1]{1,2,0:T(1,128)} %param.10) | copy-start | bytes 2548
  139.8 85.0 %copy-start.23 = (f32[16]{0:T(128)}, f32[16]{0:T(128)S(1)}, u32[]{:S(2)}) copy-start(f32[16]{0:T(128)S(1)} %compare_convert_fusion) | copy-start | bytes 196
  139.8 83.7 %copy-start.17 = (s32[1024]{0:T(1024)}, s32[1024]{0:T(1024)S(1)}, u32[]{:S(2)}) copy-start(s32[1024]{0:T(1024)S(1)} %pad_clamp_fusion) | copy-start | bytes 12292
  200.2 23.0 %all-to-all-start.1 = ((bf16[1,32,9,1024]{3,2,0,1:T(8,128)(2,1)}), bf16[1,32,9,1024]{3,2,0,1:T(8,128)(2,1)S(1)}, u32[]{:S(2)}, u32[]{:S(2)}) async-start(bf16[1,32,9,1024]{3,2,0,1:T(8,128)(2,1)} %bitcast.148), calls=%async_computation.2 | async-start | bytes 2097152 | tf_op jit(solution)/shard_map/all_to_all | solution.py:41
  207.7 117.8 %all-gather.9.cloned.1.call-start = ((), (), s32[]{:S(2)}) async-start(), calls=%async_computation.10 | async-start | bytes 1052672 | tf_op jit(solution)/shard_map/all_gather | solution.py:99
  208.8 14.7 %copy-start.18 = (f32[212]{0:T(256)}, f32[212]{0:T(256)S(1)}, u32[]{:S(2)}) copy-start(f32[212]{0:T(256)S(1)} %fusion.16) | copy-start | bytes 2548
  208.8 15.8 %copy-start.20 = (f32[212]{0:T(256)}, f32[212]{0:T(256)S(1)}, u32[]{:S(2)}) copy-start(f32[212]{0:T(256)S(1)} %add_divide_fusion) | copy-start | bytes 2548
  224.6 5.2 copy-start.2
  226.8 359.4 %copy-start.8 = (f32[1024]{0:T(1024)S(1)}, f32[1024]{0:T(1024)}, u32[]{:S(2)}) copy-start(f32[1024]{0:T(1024)} %broadcast_divide_fusion) | copy-start | bytes 12292
  226.8 359.4 %all-reduce.8.cloned.1.call-start = ((), (), s32[]{:S(2)}) async-start(), calls=%async_computation.12 | async-start | bytes 2097152
  228.4 360.6 %copy-start.24 = (f32[16]{0:T(128)S(1)}, f32[16]{0:T(128)}, u32[]{:S(2)}) copy-start(f32[16]{0:T(128)} %copy-done.23) | copy-start | bytes 196
  228.4 360.7 %copy-start.21 = (f32[212]{0:T(256)S(1)}, f32[212]{0:T(256)}, u32[]{:S(2)}) copy-start(f32[212]{0:T(256)} %copy-done.20) | copy-start | bytes 2548
  329.6 344.0 %all-gather.11.cloned.1.call-start = ((), (), s32[]{:S(2)}) async-start(), calls=%async_computation.11 | async-start | bytes 5308416 | tf_op jit(solution)/shard_map/all_gather | solution.py:27
  616.5 147.6 %reduce-scatter.5.cloned.1.call-start = ((), (), s32[]{:S(2)}) async-start(), calls=%async_computation.7 | async-start | bytes 5308416 | tf_op jit(solution)/shard_map/reduce_scatter | solution.py:34
  682.3 9.9 copy-start.26
  699.2 1.4 copy-start.6
  705.1 309.3 %all-reduce.6.cloned.1.call-start = ((), (), s32[]{:S(2)}) async-start(), calls=%async_computation.8 | async-start | bytes 262144 | tf_op jit(solution)/shard_map/psum | solution.py:133
  766.3 23.1 %all-to-all-start.3 = ((bf16[1,32,9,1024]{3,2,0,1:T(8,128)(2,1)}), bf16[1,32,9,1024]{3,2,0,1:T(8,128)(2,1)}, u32[]{:S(2)}, u32[]{:S(2)}) async-start(bf16[1,32,9,1024]{3,2,0,1:T(8,128)(2,1)} %bitcast.30), calls=%async_computation.5 | async-start | bytes 2097152 | tf_op jit(solution)/shard_map/all_to_all | solution.py:41
  780.8 12.0 %copy-start.10 = (f32[1024]{0:T(1024)S(1)}, f32[1024]{0:T(1024)}, u32[]{:S(2)}) copy-start(f32[1024]{0:T(1024)} %param.12) | copy-start | bytes 12292
  780.8 12.0 %copy-start.12 = (f32[212]{0:T(256)S(1)}, f32[212]{0:T(256)}, u32[]{:S(2)}) copy-start(f32[212]{0:T(256)} %copy-done.11) | copy-start | bytes 2548
  780.8 12.0 %copy-start.16 = (f32[212]{0:T(256)S(1)}, f32[212]{0:T(256)}, u32[]{:S(2)}) copy-start(f32[212]{0:T(256)} %copy-done.15) | copy-start | bytes 2548
  (5 other events, 5.5 us)
Sparse Core Ops, SparseCore 0:
  39.6 60.3 all-gather.6
  139.2 58.8 reduce-scatter.2
  226.9 98.4 all-gather.8
  331.3 254.8 all-reduce.7
  616.6 56.8 all-gather.10
  705.2 58.8 reduce-scatter.4
  771.1 243.2 all-reduce.5
where the time goes:
time: 1020 us
  waiting for transfers between devices  741 us (73%)
  blocking collectives  121 us (12%)
  local copies, waits for them, and re-layouts  56.6 us (6%)
  matrix products  49.8 us (5%)
  between operations  19.9 us (2%)
  other arithmetic  18.6 us (2%)
  starting transfers between devices  15.8 us (2%)
    unnamed x8, waiting for transfers between devices  255 us
    psum x1, waiting for transfers between devices, body(): lax.psum((loss_term, router_part, gain_partial_term), ('dp', 'expert'))  142 us
    all_gather x2, waiting for transfers between devices, deliver(): whole = lax.all_gather(shaped, 'dp', axis=1, tiled=True)  117 us
    reduce_scatter x2, waiting for transfers between devices, give_back(): lax.psum_scatter(partial_value.reshape(local, n_dp, n_expert * slots, wid...  108 us
    all_gather x1, waiting for transfers between devices, body(): v_all = lax.all_gather(v, ('dp', 'expert'), axis=0, tiled=True)  95.7 us
    psum x1, blocking collectives, body(): lax.psum((loss_term, router_part, gain_partial_term), ('dp', 'expert'))  75.8 us
    all_to_all x2, blocking collectives, deliver(): lax.all_to_all(buffer.reshape(experts, 1, slots, width), 'expert', split_...  45.2 us
    all_to_all x2, waiting for transfers between devices, give_back(): lax.all_to_all(rounded, 'expert', split_axis=1, concat_axis=0, tiled=True)  23 us
  transfers between devices with their start and end apart: 9, of which 9 were waited for; matrix products, arithmetic and copies ran while one was open for 3% of the time, Pallas kernels for 0%

commit v1 on v0

--- a/solution.py
+++ b/solution.py
@@ -38,7 +38,12 @@
         tiled=True,
     )
     rounded = summed.reshape(local, n_expert, slots, width)
-    returned = lax.all_to_all(rounded, "expert", split_axis=1, concat_axis=0, tiled=True)
+    returned = jnp.concatenate(
+        lax.all_to_all(
+            jnp.stack(jnp.split(rounded, lax.axis_size("expert"), axis=1)), "expert", 0, 0
+        ),
+        axis=0,
+    )
     return returned.reshape(-1, width)
 
 

time: 1020 us -> 1040 us (1.020)
  local copies, waits for them, and re-layouts: 56.6 us -> 93.9 us
  waiting for transfers between devices: 741 us -> 720 us
    unnamed x57 -> x125, local copies, waits for them, and re-layouts: 4.71 us -> 42.6 us
    psum x1, waiting for transfers between devices: 142 us -> 121 us  [body(): lax.psum((loss_term, router_part, gain_partial_term), ('dp', 'expert'))]
    another operation x3 -> x7, local copies, waits for them, and re-layouts: 19.8 us -> 22.7 us
  transfers between devices with their start and end apart: 9 -> 9, of which waited for: 9 -> 9; matrix products, arithmetic and copies ran while one was open for 3% -> 4% of each run, Pallas kernels for 0% -> 0%
where the time goes in v1:
time: 1040 us
  waiting for transfers between devices  720 us (69%)
  blocking collectives  121 us (12%)
  local copies, waits for them, and re-layouts  93.9 us (9%)
  matrix products  49.8 us (5%)
  between operations  20 us (2%)
  other arithmetic  18.6 us (2%)
  starting transfers between devices  15.8 us (2%)
    unnamed x8, waiting for transfers between devices  255 us
    psum x1, waiting for transfers between devices, body(): lax.psum((loss_term, router_part, gain_partial_term), ('dp', 'expert'))  121 us
    all_gather x2, waiting for transfers between devices, deliver(): whole = lax.all_gather(shaped, 'dp', axis=1, tiled=True)  117 us
    reduce_scatter x2, waiting for transfers between devices, give_back(): lax.psum_scatter(partial_value.reshape(local, n_dp, n_expert * slots, wid...  108 us
    all_gather x1, waiting for transfers between devices, body(): v_all = lax.all_gather(v, ('dp', 'expert'), axis=0, tiled=True)  95.7 us
    psum x1, blocking collectives, body(): lax.psum((loss_term, router_part, gain_partial_term), ('dp', 'expert'))  76 us
    all_to_all x2, blocking collectives, deliver(): lax.all_to_all(buffer.reshape(experts, 1, slots, width), 'expert', split_...  45.2 us
    unnamed x125, local copies, waits for them, and re-layouts  42.6 us
  transfers between devices with their start and end apart: 9, of which 9 were waited for; matrix products, arithmetic and copies ran while one was open for 4% of the time, Pallas kernels for 0%

profile of v1, /device:TPU:8, one launch (start us, length us, event | category | flops | bytes accessed | tf_op | source)
XLA Modules:
  0.0 1039.6 jit_solution(15475779433750570390)
XLA Ops:
  12.8 2.3 scatter_custom_fusion
  15.4 22.9 %all_to_all.28 = bf16[32,1,9,1024]{3,2,1,0:T(8,128)(2,1)S(1)} all-to-all(bf16[32,1,9,1024]{3,2,1,0:T(8,128)(2,1)S(1)} %bitcast.398), channel_id=1, replica_groups=mesh['dp'=8,'expert'=32] {'expert'}, dimensions={0} | all-to-all | bytes 1179648 | tf_op jit(solution)/shard_map/all_to_all | solution.py:23
  39.7 60.3 %all-gather.7.cloned.1.call-done = bf16[256,1,9,1024]{3,0,2,1:T(8,128)(2,1)} async-done(((bf16[32,1,9,1024]{3,0,2,1:T(8,128)(2,1)}), bf16[256,1,9,1024]{3,0,2,1:T(8,128)(2,1)}) %all-gather.7.cloned.1.call-update) | async-done | bytes 4718608 | tf_op jit(solution)/shard_map/all_gather | solution.py:27
  100.0 8.7 copy.22
  108.7 9.8 reshape.477
  118.6 14.9 %fusion.2 = (bf16[2304,512]{1,0:T(8,128)(2,1)S(1)}, f32[2304,512]{1,0:T(8,128)}) fusion(bf16[2304,1024]{1,0:T(8,128)(2,1)} %reshape.477, bf16[1,1024,512]{2,1,0:T(8,128)(2,1)S(1)} %copy-done), kind=kOutput, calls=%fused_computation.9 | convolution fusion | flops 2492596224 | bytes 12845056 | tf_op jit(solution)/shard_map/erd,edf->erf/dot_general | solution.py:81
  133.4 1.4 copy-done.30
  134.8 4.2 convert_bitcast_fusion.1
  139.8 58.3 %reduce-scatter.3.cloned.1.call-done = bf16[1,1,288,1024]{3,2,1,0:T(8,128)(2,1)} async-done(((bf16[1,8,288,1024]{3,2,1,0:T(8,128)(2,1)}), bf16[1,1,288,1024]{3,2,1,0:T(8,128)(2,1)}) %reduce-scatter.3.cloned.1.call-update) | async-done | bytes 589840 | tf_op jit(solution)/shard_map/reduce_scatter | solution.py:34
  219.1 7.4 all-to-all-start.1
  227.7 14.4 %all-to-all-done.1 = bf16[32,1,1,9,1024]{4,3,2,1,0:T(8,128)(2,1)S(1)} async-done(((bf16[32,1,1,9,1024]{4,3,2,1,0:T(8,128)(2,1)}), bf16[32,1,1,9,1024]{4,3,2,1,0:T(8,128)(2,1)S(1)}, u32[]{:S(2)}, u32[]{:S(2)}) %all-to-all-start.1) | async-done | bytes 589856 | tf_op jit(solution)/shard_map/all_to_all | solution.py:42
  248.7 95.7 %all-gather.9.cloned.1.call-done = f32[262144]{0:T(1024)} async-done(((f32[1024]{0:T(1024)}), f32[262144]{0:T(1024)}) %all-gather.9.cloned.1.call-update) | async-done | bytes 1048592 | tf_op jit(solution)/shard_map/all_gather | solution.py:104
  350.4 254.7 %all-reduce.8.cloned.1.call-done = f32[256,1024]{1,0:T(8,128)} async-done(((f32[256,1024]{1,0:T(8,128)}), f32[256,1024]{1,0:T(8,128)}) %all-reduce.8.cloned.1.call-update) | async-done | bytes 1048592
  608.1 2.5 scatter_custom_fusion.1
  611.9 22.3 %all_to_all.29 = bf16[32,1,9,1024]{3,2,1,0:T(8,128)(2,1)S(1)} all-to-all(bf16[32,1,9,1024]{3,2,1,0:T(8,128)(2,1)S(1)} %bitcast.399), channel_id=1, replica_groups=mesh['dp'=8,'expert'=32] {'expert'}, dimensions={0} | all-to-all | bytes 1179648 | tf_op jit(solution)/shard_map/all_to_all | solution.py:23
  635.5 57.0 %all-gather.11.cloned.1.call-done = bf16[256,1,9,1024]{3,0,2,1:T(8,128)(2,1)} async-done(((bf16[32,1,9,1024]{3,0,2,1:T(8,128)(2,1)}), bf16[256,1,9,1024]{3,0,2,1:T(8,128)(2,1)}) %all-gather.11.cloned.1.call-update) | async-done | bytes 4718608 | tf_op jit(solution)/shard_map/all_gather | solution.py:27
  692.5 8.7 copy.25
  701.2 9.9 reshape.485
  711.1 7.0 fusion.14
  718.1 1.4 copy-done.6
  719.5 4.4 convert_bitcast_fusion
  726.2 7.0 convolution_bitcast_fusion
  733.2 49.8 %reduce-scatter.5.cloned.1.call-done = bf16[1,1,288,1024]{3,2,1,0:T(8,128)(2,1)} async-done(((bf16[1,8,288,1024]{3,2,1,0:T(8,128)(2,1)}), bf16[1,1,288,1024]{3,2,1,0:T(8,128)(2,1)}) %reduce-scatter.5.cloned.1.call-update) | async-done | bytes 589840 | tf_op jit(solution)/shard_map/reduce_scatter | solution.py:34
  803.7 7.5 all-to-all-start.3
  811.1 7.1 convolution_bitcast_fusion.1
  818.2 8.6 all-to-all-done.3
  826.8 1.4 reshape_reshape.7
  828.3 2.0 gather_fusion.1
  830.3 2.3 fusion.37
  833.7 76.0 %all-reduce.2 = (f32[1]{0:T(128)}, f32[1024]{0:T(1024)}) all-reduce(f32[1]{0:T(128)} %bitcast.51, f32[1024]{0:T(1024)S(1)} %get-tuple-element.6), channel_id=1, replica_groups=mesh['dp'=8,'expert'=32] {'dp','expert'}, use_global_device_ids=true, to_apply=%region_13.14 | all-reduce | flops 1025 | bytes 8200 | tf_op jit(solution)/shard_map/psum | solution.py:138
  909.8 121.4 %all-reduce.6.cloned.1.call-done = f32[1024,32]{0,1:T(8,128)} async-done(((f32[1024,32]{0,1:T(8,128)}), f32[1024,32]{0,1:T(8,128)}) %all-reduce.6.cloned.1.call-update) | async-done | bytes 131088 | tf_op jit(solution)/shard_map/psum | solution.py:138
  1031.1 1.6 copy.97
  (187 shorter events, 66.7 us)
Async XLA Ops:
  7.2 111.4 %copy-start = (bf16[1,1024,512]{2,1,0:T(8,128)(2,1)S(1)}, bf16[1,1024,512]{2,1,0:T(8,128)(2,1)}, u32[]{:S(2)}) copy-start(bf16[1,1024,512]{2,1,0:T(8,128)(2,1)} %param.14) | copy-start | bytes 3145732
  7.2 92.8 %all-gather.7.cloned.1.call-start = ((), (), s32[]{:S(2)}) async-start(), calls=%async_computation.9 | async-start | bytes 5308416 | tf_op jit(solution)/shard_map/all_gather | solution.py:27
  8.5 218.1 %copy-start.11 = (f32[212]{0:T(256)}, f32[212]{0:T(256)S(1)}, u32[]{:S(2)}) copy-start(f32[212]{0:T(256)S(1)} %broadcast_multiply_fusion.3) | copy-start | bytes 2548
  9.8 216.9 %copy-start.16 = (f32[212]{0:T(256)}, f32[212]{0:T(256)S(1)}, u32[]{:S(2)}) copy-start(f32[212]{0:T(256)S(1)} %add_rsqrt_fusion) | copy-start | bytes 2548
  12.8 127.0 %copy-start.25 = (s32[212,1]{0,1:T(1,128)}, s32[212,1]{0,1:T(1,128)S(1)}, u32[]{:S(2)}) copy-start(s32[212,1]{0,1:T(1,128)S(1)} %compare_select_fusion) | copy-start | bytes 2548
  39.4 158.6 %reduce-scatter.3.cloned.1.call-start = ((), (), s32[]{:S(2)}) async-start(), calls=%async_computation.6 | async-start | bytes 5308416 | tf_op jit(solution)/shard_map/reduce_scatter | solution.py:34
  118.6 16.3 %copy-start.28 = (bf16[1,512,1024]{2,1,0:T(8,128)(2,1)S(1)}, bf16[1,512,1024]{2,1,0:T(8,128)(2,1)}, u32[]{:S(2)}) copy-start(bf16[1,512,1024]{2,1,0:T(8,128)(2,1)} %param.15) | copy-start | bytes 3145732
  139.0 87.6 %copy-start.1 = (bf16[1,212,1024]{2,1,0:T(8,128)(2,1)S(1)}, bf16[1,212,1024]{2,1,0:T(8,128)(2,1)}, u32[]{:S(2)}) copy-start(bf16[1,212,1024]{2,1,0:T(8,128)(2,1)} %param.9) | copy-start | bytes 1302532
  139.0 87.6 %copy-start.9 = (f32[1024]{0:T(1024)S(1)}, f32[1024]{0:T(1024)}, u32[]{:S(2)}) copy-start(f32[1024]{0:T(1024)} %param.12) | copy-start | bytes 12292
  139.0 87.9 %copy-start.7 = (f32[1024,32]{0,1:T(8,128)S(1)}, f32[1024,32]{0,1:T(8,128)}, u32[]{:S(2)}) copy-start(f32[1024,32]{0,1:T(8,128)} %param.13) | copy-start | bytes 393220
  139.0 87.9 %copy-start.13 = (s32[1,212,1]{1,2,0:T(1,128)S(1)}, s32[1,212,1]{1,2,0:T(1,128)}, u32[]{:S(2)}) copy-start(s32[1,212,1]{1,2,0:T(1,128)} %param.10) | copy-start | bytes 2548
  139.8 103.9 %copy-start.26 = (f32[16]{0:T(128)}, f32[16]{0:T(128)S(1)}, u32[]{:S(2)}) copy-start(f32[16]{0:T(128)S(1)} %compare_convert_fusion) | copy-start | bytes 196
  139.8 102.6 %copy-start.18 = (s32[1024]{0:T(1024)}, s32[1024]{0:T(1024)S(1)}, u32[]{:S(2)}) copy-start(s32[1024]{0:T(1024)S(1)} %pad_clamp_fusion) | copy-start | bytes 12292
  219.1 23.0 %all-to-all-start.1 = ((bf16[32,1,1,9,1024]{4,3,2,1,0:T(8,128)(2,1)}), bf16[32,1,1,9,1024]{4,3,2,1,0:T(8,128)(2,1)S(1)}, u32[]{:S(2)}, u32[]{:S(2)}) async-start(bf16[32,1,1,9,1024]{4,3,2,1,0:T(8,128)(2,1)} %constant_dynamic-update-slice_fusion), calls=%async_computation.2 | async-start | bytes 2097152 | tf_op jit(solution)/shard_map/all_to_all | solution.py:42
  226.6 117.8 %all-gather.9.cloned.1.call-start = ((), (), s32[]{:S(2)}) async-start(), calls=%async_computation.10 | async-start | bytes 1052672 | tf_op jit(solution)/shard_map/all_gather | solution.py:104
  227.7 14.7 %copy-start.19 = (f32[212]{0:T(256)}, f32[212]{0:T(256)S(1)}, u32[]{:S(2)}) copy-start(f32[212]{0:T(256)S(1)} %fusion.16) | copy-start | bytes 2548
  227.7 15.8 %copy-start.21 = (f32[212]{0:T(256)}, f32[212]{0:T(256)S(1)}, u32[]{:S(2)}) copy-start(f32[212]{0:T(256)S(1)} %add_divide_fusion) | copy-start | bytes 2548
  245.7 359.4 %copy-start.8 = (f32[1024]{0:T(1024)S(1)}, f32[1024]{0:T(1024)}, u32[]{:S(2)}) copy-start(f32[1024]{0:T(1024)} %broadcast_divide_fusion) | copy-start | bytes 12292
  245.7 359.4 %all-reduce.8.cloned.1.call-start = ((), (), s32[]{:S(2)}) async-start(), calls=%async_computation.12 | async-start | bytes 2097152
  247.3 360.6 %copy-start.27 = (f32[16]{0:T(128)S(1)}, f32[16]{0:T(128)}, u32[]{:S(2)}) copy-start(f32[16]{0:T(128)} %copy-done.26) | copy-start | bytes 196
  247.4 360.7 %copy-start.22 = (f32[212]{0:T(256)S(1)}, f32[212]{0:T(256)}, u32[]{:S(2)}) copy-start(f32[212]{0:T(256)} %copy-done.21) | copy-start | bytes 2548
  348.5 344.0 %all-gather.11.cloned.1.call-start = ((), (), s32[]{:S(2)}) async-start(), calls=%async_computation.11 | async-start | bytes 5308416 | tf_op jit(solution)/shard_map/all_gather | solution.py:27
  635.4 147.6 %reduce-scatter.5.cloned.1.call-start = ((), (), s32[]{:S(2)}) async-start(), calls=%async_computation.7 | async-start | bytes 5308416 | tf_op jit(solution)/shard_map/reduce_scatter | solution.py:34
  701.2 9.9 copy-start.29
  724.0 307.2 %all-reduce.6.cloned.1.call-start = ((), (), s32[]{:S(2)}) async-start(), calls=%async_computation.8 | async-start | bytes 262144 | tf_op jit(solution)/shard_map/psum | solution.py:138
  725.2 8.0 copy-start.23
  803.7 23.1 %all-to-all-start.3 = ((bf16[32,1,1,9,1024]{4,3,2,1,0:T(8,128)(2,1)}), bf16[32,1,1,9,1024]{4,3,2,1,0:T(8,128)(2,1)}, u32[]{:S(2)}, u32[]{:S(2)}) async-start(bf16[32,1,1,9,1024]{4,3,2,1,0:T(8,128)(2,1)} %constant_dynamic-update-slice_fusion.32), calls=%async_computation.5 | async-start | bytes 2097152 | tf_op jit(solution)/shard_map/all_to_all | solution.py:42
  818.2 12.0 %copy-start.10 = (f32[1024]{0:T(1024)S(1)}, f32[1024]{0:T(1024)}, u32[]{:S(2)}) copy-start(f32[1024]{0:T(1024)} %param.12) | copy-start | bytes 12292
  818.2 12.0 %copy-start.12 = (f32[212]{0:T(256)S(1)}, f32[212]{0:T(256)}, u32[]{:S(2)}) copy-start(f32[212]{0:T(256)} %copy-done.11) | copy-start | bytes 2548
  818.2 12.0 %copy-start.15 = (s32[1,212,1]{1,2,0:T(1,128)S(1)}, s32[1,212,1]{1,2,0:T(1,128)}, u32[]{:S(2)}) copy-start(s32[1,212,1]{1,2,0:T(1,128)} %param.10) | copy-start | bytes 2548
  818.2 12.0 %copy-start.17 = (f32[212]{0:T(256)S(1)}, f32[212]{0:T(256)}, u32[]{:S(2)}) copy-start(f32[212]{0:T(256)} %copy-done.16) | copy-start | bytes 2548
  818.2 12.1 %copy-start.24 = (f32[212]{0:T(256)S(1)}, f32[212]{0:T(256)}, u32[]{:S(2)}) copy-start(f32[212]{0:T(256)} %copy-done.23) | copy-start | bytes 2548
  (8 other events, 13.5 us)
Sparse Core Ops, SparseCore 0:
  39.6 60.3 all-gather.6
  139.2 58.8 reduce-scatter.2
  245.8 98.4 all-gather.8
  350.2 254.8 all-reduce.7
  635.6 56.8 all-gather.10
  724.1 58.8 reduce-scatter.4
  790.0 241.1 all-reduce.5
